TPU v7x, 32 devices: a whole 2x2x4 slice. The times are simulated.
32 devices in a mesh: chan: 8 (over y, x, core), band: 4 (over z).
Axes of the slice: x: 2, y: 2, z: 4, core: 2. Of those that a mesh axis runs over, the one named last changes fastest.
Arguments:
- spectra: bfloat16 [96, 2048, 384], P('band', 'chan')
- half_width: int32 [2048], P('chan'), may hold values from 4 to 12
- partner: int32 [2, 8], replicated, may hold values from 0 to 7, as said below
Outputs:
- cross: bfloat16 [3, 96, 2048, 512], P(None, 'band', 'chan')
Inputs may be any that keep to these rules, and one draw needn't show every extreme that they name: Each row pairs the blocks: partner[r, partner[r, a]] = a and partner[r, a] != a; no two rows pair the same two blocks.
All inputs are finite; a program needn't handle non-finite values.
Results may differ from a plain program's by a relative error of at most 0.0056.
Values may be sent and summed in bfloat16 or wider, within the bound.
No kernel may reach another device: no remote copies, remote signals or barrier semaphores. Data moves between devices by JAX's collectives and lax.ppermute only.
A program may use at most 128 MiB of HBM per device.

v0:
```python
import jax
import jax.numpy as jnp
from jax import lax
from jax.sharding import PartitionSpec as P

HMAX = 12
ROUNDS = 2


def padded_2(cells, sides, width):
    for axis, dim in sides:
        count = lax.axis_size(axis)
        ends = count - 1
        head = lax.slice_in_dim(cells, 0, width, axis=dim)
        tail = lax.slice_in_dim(cells, cells.shape[dim] - width, cells.shape[dim], axis=dim)
        cells = jnp.concatenate(
            [
                lax.ppermute(tail, axis, [(i, (i + 1) % count) for i in range(ends)]),
                cells,
                lax.ppermute(head, axis, [((i + 1) % count, i) for i in range(ends)]),
            ],
            axis=dim,
        )
    return cells


def pair_block(own, other, windows):
    turned = jnp.concatenate([-other[:, :, windows:], other[:, :, :windows]], axis=2)
    right = jnp.concatenate([other, turned], axis=1)
    product = jnp.einsum("fcw,fdw->fcd", own, right, preferred_element_type=jnp.float32)
    return (product * (1.0 / windows)).astype(jnp.bfloat16)


def body(spectra, half_width, partner):
    bins, chans, columns = spectra.shape
    windows = columns // 2
    raw = spectra.astype(jnp.float32)
    power = jnp.sum(raw * raw, axis=2)
    padded = padded_2(power, (("band", 0),), HMAX)
    first = lax.axis_index("band") * bins - HMAX
    position = first + jnp.arange(bins + 2 * HMAX, dtype=jnp.int32)
    present = ((position >= 0) & (position < bins * lax.axis_size("band"))).astype(jnp.float32)[
        :, None
    ]
    total = jnp.zeros((bins, chans), jnp.float32)
    count = jnp.zeros((bins, chans), jnp.float32)
    for offset in range(-HMAX, HMAX + 1):
        inside = (abs(offset) <= half_width).astype(jnp.float32)[None, :]
        total = total + padded[HMAX + offset : HMAX + offset + bins] * inside
        count = count + present[HMAX + offset : HMAX + offset + bins] * inside
    scale = lax.rsqrt(total / (2.0 * windows * count) + 1e-06)
    white = (raw * scale[:, :, None]).astype(jnp.bfloat16)
    blocks = lax.axis_size("chan")
    piece = chans // blocks
    sectioned = white.reshape(bins, blocks, piece, columns)
    results = [pair_block(white, white, windows)]
    for step in range(ROUNDS):
        held = lax.all_to_all(sectioned, "chan", split_axis=1, concat_axis=1, tiled=True)
        chosen = jnp.take(held, partner[step], axis=1)
        other = lax.all_to_all(chosen, "chan", split_axis=1, concat_axis=1, tiled=True)
        results.append(pair_block(white, other.reshape(bins, chans, columns), windows))
    return jnp.stack(results)


def solution(mesh):
    placed = (P("band", "chan", None), P("chan"), P())
    return jax.shard_map(
        body, mesh=mesh, in_specs=placed, out_specs=P(None, "band", "chan", None), check_vma=False
    )
```

profile of v0, /device:TPU:0, one launch (start us, length us, event | category | flops | bytes accessed | tf_op | source)
XLA Modules:
  0.0 252.5 jit_solution(4837852159365645081)
XLA Ops:
  0.0 0.0 copy-start.3
  0.0 3.4 %fusion = f32[24,256]{1,0:T(8,128)S(1)} fusion(bf16[24,256,384]{2,1,0:T(8,128)(2,1)} %param.5), kind=kLoop, calls=%fused_computation.8 | loop fusion | flops 7071744 | bytes 4743168 | tf_op jit(solution)/shard_map/reduce_sum | solution.py:38
  3.4 5.0 %collective-permute-start = (f32[12,256]{1,0:T(8,128)S(1)}, f32[12,256]{1,0:T(8,128)S(1)}, u32[]{:S(2)}, u32[]{:S(2)}) collective-permute-start(f32[12,256]{1,0:T(8,128)S(1)} %get-tuple-element.16), channel_id=1, source_target_pairs={{0,1},{1,2},{2,3},{4,5},{5,6},{6,7},{8,9},{9,10},{10,11},{12,13},{... | collective-permute-start | bytes 36872 | tf_op jit(solution)/shard_map/ppermute | solution.py:18
  8.3 1.3 collective-permute-start.1
  9.7 0.1 fusion.106
  9.7 0.0 copy-done.3
  9.8 0.1 fusion.107
  9.8 0.0 collective-permute-done
  9.8 4.1 %collective-permute-done.1 = f32[12,256]{1,0:T(8,128)S(1)} collective-permute-done((f32[12,256]{1,0:T(8,128)S(1)}, f32[12,256]{1,0:T(8,128)S(1)}, u32[]{:S(2)}, u32[]{:S(2)}) %collective-permute-start.1) | collective-permute-done | bytes 12320 | tf_op jit(solution)/shard_map/ppermute | solution.py:20
  14.0 0.2 fusion.101
  14.2 2.9 %fusion.1 = bf16[24,256,384]{2,1,0:T(8,128)(2,1)S(1)} fusion(bf16[24,256,384]{2,1,0:T(8,128)(2,1)} %param.5, f32[24,256]{1,0:T(8,128)S(1)} %fusion.101), kind=kLoop, calls=%fused_computation.9 | loop fusion | flops 7077888 | bytes 9461760 | tf_op jit(solution)/shard_map/convert_element_type | solution.py:52
  17.1 0.0 copy-start
  17.1 2.2 copy-done
  19.3 2.7 %copy.6 = bf16[24,8,32,384]{3,2,0,1:T(8,128)(2,1)} copy(bf16[24,8,32,384]{3,2,1,0:T(8,128)(2,1)S(1)} %bitcast.22) | data formatting | bytes 9437184 | tf_op jit(solution)/shard_map/reshape | solution.py:55
  22.0 0.0 copy-start.4
  22.0 4.7 %all-to-all-start = ((bf16[24,8,32,384]{3,2,0,1:T(8,128)(2,1)}), bf16[24,8,32,384]{3,2,0,1:T(8,128)(2,1)}, u32[]{:S(2)}, u32[]{:S(2)}) async-start(bf16[24,8,32,384]{3,2,0,1:T(8,128)(2,1)} %copy.6), calls=%async_computation | async-start | bytes 9437184 | tf_op jit(solution)/shard_map/all_to_all | solution.py:58
  26.7 0.0 copy-done.4
  26.8 54.7 %all-to-all-done = bf16[24,8,32,384]{3,2,0,1:T(8,128)(2,1)} async-done(((bf16[24,8,32,384]{3,2,0,1:T(8,128)(2,1)}), bf16[24,8,32,384]{3,2,0,1:T(8,128)(2,1)}, u32[]{:S(2)}, u32[]{:S(2)}) %all-to-all-start) | async-done | bytes 4718624 | tf_op jit(solution)/shard_map/all_to_all | solution.py:58
  81.4 5.7 %gather_fusion = bf16[8,24,32,384]{3,2,1,0:T(8,128)(2,1)} fusion(bf16[24,8,32,384]{3,2,0,1:T(8,128)(2,1)} %all-to-all-done, s32[1024]{0:T(1024)S(1)} %pad_clamp_fusion.1), kind=kCustom, calls=%fused_computation.clone | custom fusion | bytes 9437216 | tf_op jit(solution)/shard_map/jit(_take)/gather | solution.py:59
  87.1 5.1 %select_bitcast_fusion.1 = bf16[24,8,32,384]{3,2,0,1:T(8,128)(2,1)} fusion(bf16[8,24,32,384]{3,2,1,0:T(8,128)(2,1)} %gather_fusion, pred[8]{0:T(512)(128)(4,1)S(1)} %get-tuple-element.6), kind=kLoop, calls=%fused_computation.32 | loop fusion | flops 2359296 | bytes 9437192 | tf_op jit(solution)/shard_map/jit(_take)/select_n | solution.py:59
  92.2 4.6 %all-to-all-start.1 = ((bf16[24,8,32,384]{3,2,0,1:T(8,128)(2,1)}), bf16[24,8,32,384]{3,2,0,1:T(8,128)(2,1)}, u32[]{:S(2)}, u32[]{:S(2)}) async-start(bf16[24,8,32,384]{3,2,0,1:T(8,128)(2,1)} %select_bitcast_fusion.1), calls=%async_computation.1 | async-start | bytes 9437184 | tf_op jit(solution)/shard_map/all_to_all | solution.py:60
  96.8 5.8 %gather_fusion.1 = bf16[8,24,32,384]{3,2,1,0:T(8,128)(2,1)} fusion(bf16[24,8,32,384]{3,2,0,1:T(8,128)(2,1)} %all-to-all-done, s32[1024]{0:T(1024)S(1)} %pad_clamp_fusion), kind=kCustom, calls=%fused_computation.1.clone | custom fusion | bytes 9437216 | tf_op jit(solution)/shard_map/jit(_take)/gather | solution.py:59
  102.6 5.2 %select_bitcast_fusion = bf16[24,8,32,384]{3,2,0,1:T(8,128)(2,1)} fusion(bf16[8,24,32,384]{3,2,1,0:T(8,128)(2,1)} %gather_fusion.1, pred[8]{0:T(512)(128)(4,1)S(1)} %get-tuple-element.18), kind=kLoop, calls=%fused_computation.31 | loop fusion | flops 2359296 | bytes 9437192 | tf_op jit(solution)/shard_map/jit(_take)/select_n | solution.py:59
  107.8 43.7 %all-to-all-done.1 = bf16[24,8,32,384]{3,2,0,1:T(8,128)(2,1)} async-done(((bf16[24,8,32,384]{3,2,0,1:T(8,128)(2,1)}), bf16[24,8,32,384]{3,2,0,1:T(8,128)(2,1)}, u32[]{:S(2)}, u32[]{:S(2)}) %all-to-all-start.1) | async-done | bytes 4718624 | tf_op jit(solution)/shard_map/all_to_all | solution.py:60
  151.5 0.0 slice-start
  151.5 4.9 %all-to-all-start.2 = ((bf16[24,8,32,384]{3,2,0,1:T(8,128)(2,1)}), bf16[24,8,32,384]{3,2,0,1:T(8,128)(2,1)}, u32[]{:S(2)}, u32[]{:S(2)}) async-start(bf16[24,8,32,384]{3,2,0,1:T(8,128)(2,1)} %select_bitcast_fusion), calls=%async_computation.2 | async-start | bytes 9437184 | tf_op jit(solution)/shard_map/all_to_all | solution.py:60
  156.5 0.0 slice-start.1
  156.5 6.6 %slice_negate_fusion.2 = (bf16[24,256,192]{2,1,0:T(8,128)(2,1)}, bf16[24,256,192]{2,1,0:T(8,128)(2,1)}) fusion(bf16[24,256,384]{2,1,0:T(8,128)(2,1)} %copy-done), kind=kLoop, calls=%fused_computation.35 | loop fusion | flops 1179648 | bytes 9437184 | tf_op jit(solution)/shard_map/neg | solution.py:28
  163.1 0.0 slice-done
  163.1 0.0 slice-done.1
  163.1 8.0 %fusion.20 = bf16[1,24,256,512]{3,2,1,0:T(8,128)(2,1)} fusion(bf16[24,256,384]{2,1,0:T(8,128)(2,1)S(1)} %bitcast.24, bf16[24,256,192]{2,1,0:T(8,128)(2,1)} %get-tuple-element.11, bf16[24,256,192]{2,1,0:T(8,128)(2,1)} %get-tuple-element.10), kind=kOutput, calls=%fused_computation.28 | convolution fusion | flops 2450522112 | bytes 15728640 | tf_op jit(solution)/shard_map/fcw,fdw->fcd/dot_general | solution.py:30
  171.2 3.2 %copy.7 = bf16[24,8,32,384]{3,2,1,0:T(8,128)(2,1)S(1)} copy(bf16[24,8,32,384]{3,2,0,1:T(8,128)(2,1)} %all-to-all-done.1) | data formatting | bytes 9437184 | tf_op jit(solution)/shard_map/all_to_all | solution.py:60
  174.4 0.0 copy-start.1
  174.4 2.2 copy-done.1
  176.5 3.7 %slice_negate_fusion.1 = (bf16[24,256,192]{2,1,0:T(8,128)(2,1)}, bf16[24,256,192]{2,1,0:T(8,128)(2,1)}) fusion(bf16[24,256,384]{2,1,0:T(8,128)(2,1)S(1)} %bitcast.27), kind=kLoop, calls=%fused_computation.34 | loop fusion | flops 1179648 | bytes 9437184 | tf_op jit(solution)/shard_map/neg | solution.py:28
  180.3 30.7 %all-to-all-done.2 = bf16[24,8,32,384]{3,2,0,1:T(8,128)(2,1)} async-done(((bf16[24,8,32,384]{3,2,0,1:T(8,128)(2,1)}), bf16[24,8,32,384]{3,2,0,1:T(8,128)(2,1)}, u32[]{:S(2)}, u32[]{:S(2)}) %all-to-all-start.2) | async-done | bytes 4718624 | tf_op jit(solution)/shard_map/all_to_all | solution.py:60
  211.0 0.0 slice-start.2
  211.0 3.3 %copy.8 = bf16[24,8,32,384]{3,2,1,0:T(8,128)(2,1)S(1)} copy(bf16[24,8,32,384]{3,2,0,1:T(8,128)(2,1)} %all-to-all-done.2) | data formatting | bytes 9437184 | tf_op jit(solution)/shard_map/all_to_all | solution.py:60
  214.3 0.0 copy-start.2
  214.4 0.0 slice-start.3
  214.4 4.0 %slice_negate_fusion = (bf16[24,256,192]{2,1,0:T(8,128)(2,1)}, bf16[24,256,192]{2,1,0:T(8,128)(2,1)}) fusion(bf16[24,256,384]{2,1,0:T(8,128)(2,1)S(1)} %bitcast.29), kind=kLoop, calls=%fused_computation.33 | loop fusion | flops 1179648 | bytes 9437184 | tf_op jit(solution)/shard_map/neg | solution.py:28
  218.4 0.0 copy-done.2
  218.4 0.0 slice-done.2
  218.4 0.0 slice-done.3
  218.4 8.8 %fusion.21 = bf16[1,24,256,512]{3,2,1,0:T(8,128)(2,1)} fusion(bf16[24,256,384]{2,1,0:T(8,128)(2,1)S(1)} %bitcast.26, bf16[24,256,192]{2,1,0:T(8,128)(2,1)} %get-tuple-element.13, bf16[24,256,192]{2,1,0:T(8,128)(2,1)} %get-tuple-element.12, bf16[24,256,384]{2,1,0:T(8,128)(2,1)} %bitcast.28), kind=kOutput, calls=%fused_computation.29 | convolution fusion | flops 2450522112 | bytes 20447232 | tf_op jit(solution)/shard_map/fcw,fdw->fcd/dot_general | solution.py:30
  227.2 8.8 %fusion.22 = bf16[1,24,256,512]{3,2,1,0:T(8,128)(2,1)} fusion(bf16[24,256,384]{2,1,0:T(8,128)(2,1)S(1)} %bitcast.26, bf16[24,256,192]{2,1,0:T(8,128)(2,1)} %get-tuple-element.15, bf16[24,256,192]{2,1,0:T(8,128)(2,1)} %get-tuple-element.14, bf16[24,256,384]{2,1,0:T(8,128)(2,1)} %bitcast.30), kind=kOutput, calls=%fused_computation.30 | convolution fusion | flops 2450522112 | bytes 20447232 | tf_op jit(solution)/shard_map/fcw,fdw->fcd/dot_general | solution.py:30
  236.0 16.5 %pad_maximum_fusion = bf16[3,24,256,512]{3,2,1,0:T(8,128)(2,1)} fusion(bf16[1,24,256,512]{3,2,1,0:T(8,128)(2,1)} %fusion.22, bf16[1,24,256,512]{3,2,1,0:T(8,128)(2,1)} %fusion.21, bf16[1,24,256,512]{3,2,1,0:T(8,128)(2,1)} %fusion.20), kind=kLoop, calls=%fused_computation.2 | loop fusion | flops 18874368 | bytes 37748736 | tf_op jit(solution)/shard_map/stack | solution.py:62
  (8 shorter events, 0.0 us)
Async XLA Ops:
  0.0 9.7 %copy-start.3 = (s32[256]{0:T(256)S(1)}, s32[256]{0:T(256)}, u32[]{:S(2)}) copy-start(s32[256]{0:T(256)} %param.6) | copy-start | bytes 3076
  3.4 6.5 %collective-permute-start = (f32[12,256]{1,0:T(8,128)S(1)}, f32[12,256]{1,0:T(8,128)S(1)}, u32[]{:S(2)}, u32[]{:S(2)}) collective-permute-start(f32[12,256]{1,0:T(8,128)S(1)} %get-tuple-element.16), channel_id=1, source_target_pairs={{0,1},{1,2},{2,3},{4,5},{5,6},{6,7},{8,9},{9,10},{10,11},{12,13},{... | collective-permute-start | bytes 36872 | tf_op jit(solution)/shard_map/ppermute | solution.py:18
  8.3 5.6 %collective-permute-start.1 = (f32[12,256]{1,0:T(8,128)S(1)}, f32[12,256]{1,0:T(8,128)S(1)}, u32[]{:S(2)}, u32[]{:S(2)}) collective-permute-start(f32[12,256]{1,0:T(8,128)S(1)} %get-tuple-element.17), channel_id=1, source_target_pairs={{1,0},{2,1},{3,2},{5,4},{6,5},{7,6},{9,8},{10,9},{11,10},{13,12},{... | collective-permute-start | bytes 36872 | tf_op jit(solution)/shard_map/ppermute | solution.py:20
  17.1 2.2 copy-start
  22.0 4.8 %copy-start.4 = (s32[2,8]{1,0:T(2,128)S(1)}, s32[2,8]{1,0:T(2,128)}, u32[]{:S(2)}) copy-start(s32[2,8]{1,0:T(2,128)} %param.7) | copy-start | bytes 196
  22.0 59.5 %all-to-all-start = ((bf16[24,8,32,384]{3,2,0,1:T(8,128)(2,1)}), bf16[24,8,32,384]{3,2,0,1:T(8,128)(2,1)}, u32[]{:S(2)}, u32[]{:S(2)}) async-start(bf16[24,8,32,384]{3,2,0,1:T(8,128)(2,1)} %copy.6), calls=%async_computation | async-start | bytes 9437184 | tf_op jit(solution)/shard_map/all_to_all | solution.py:58
  92.2 59.3 %all-to-all-start.1 = ((bf16[24,8,32,384]{3,2,0,1:T(8,128)(2,1)}), bf16[24,8,32,384]{3,2,0,1:T(8,128)(2,1)}, u32[]{:S(2)}, u32[]{:S(2)}) async-start(bf16[24,8,32,384]{3,2,0,1:T(8,128)(2,1)} %select_bitcast_fusion.1), calls=%async_computation.1 | async-start | bytes 9437184 | tf_op jit(solution)/shard_map/all_to_all | solution.py:60
  151.5 11.6 %slice-start = ((s8[4718592]{0:T(1024)(128)(4,1)}), s8[524288]{0:T(1024)(128)(4,1)S(1)}, s32[]{:S(2)}) async-start(s8[4718592]{0:T(1024)(128)(4,1)} %bitcast.23), calls=%async_computation.3 | async-start | bytes 1048576
  151.5 59.5 %all-to-all-start.2 = ((bf16[24,8,32,384]{3,2,0,1:T(8,128)(2,1)}), bf16[24,8,32,384]{3,2,0,1:T(8,128)(2,1)}, u32[]{:S(2)}, u32[]{:S(2)}) async-start(bf16[24,8,32,384]{3,2,0,1:T(8,128)(2,1)} %select_bitcast_fusion), calls=%async_computation.2 | async-start | bytes 9437184 | tf_op jit(solution)/shard_map/all_to_all | solution.py:60
  156.5 6.7 %slice-start.1 = ((s8[4718592]{0:T(1024)(128)(4,1)}), s8[4194304]{0:T(1024)(128)(4,1)S(1)}, s32[]{:S(2)}) async-start(s8[4718592]{0:T(1024)(128)(4,1)} %bitcast.23), calls=%async_computation.4 | async-start | bytes 8388608
  174.4 2.2 copy-start.1
  211.0 7.4 %slice-start.2 = ((s8[4718592]{0:T(1024)(128)(4,1)}), s8[4194304]{0:T(1024)(128)(4,1)S(1)}, s32[]{:S(2)}) async-start(s8[4718592]{0:T(1024)(128)(4,1)} %bitcast.25), calls=%async_computation.5 | async-start | bytes 8388608
  214.3 4.1 %copy-start.2 = (bf16[24,8,32,384]{3,2,1,0:T(8,128)(2,1)}, bf16[24,8,32,384]{3,2,1,0:T(8,128)(2,1)S(1)}, u32[]{:S(2)}) copy-start(bf16[24,8,32,384]{3,2,1,0:T(8,128)(2,1)S(1)} %copy.8) | copy-start | bytes 14155780
  214.4 4.1 %slice-start.3 = ((s8[4718592]{0:T(1024)(128)(4,1)}), s8[524288]{0:T(1024)(128)(4,1)S(1)}, s32[]{:S(2)}) async-start(s8[4718592]{0:T(1024)(128)(4,1)} %bitcast.25), calls=%async_computation.6 | async-start | bytes 1048576
where the time goes:
time: 253 us
  waiting for transfers between devices  133 us (53%)
  other arithmetic  47.6 us (19%)
  matrix products  25.6 us (10%)
  local copies, waits for them, and re-layouts  25.3 us (10%)
  starting transfers between devices  20.5 us (8%)
    all_to_all x2, waiting for transfers between devices, body(): lax.all_to_all(chosen, 'chan', split_axis=1, concat_axis=1, tiled=True)  74.5 us
    all_to_all x1, waiting for transfers between devices, body(): lax.all_to_all(sectioned, 'chan', split_axis=1, concat_axis=1, tiled=True)  54.7 us
    dot_general x3, matrix products, pair_block(): jnp.einsum('fcw,fdw->fcd', own, right, preferred_element_type=jnp.float32)  25.6 us
    another operation x1, other arithmetic, body(): return jnp.stack(results)  16.5 us
    neg x3, other arithmetic, pair_block(): -other[:, :, windows:]  14.4 us
    gather x2, local copies, waits for them, and re-layouts, body(): chosen = jnp.take(held, partner[step], axis=1)  11.5 us
    select_n x2, other arithmetic, body(): chosen = jnp.take(held, partner[step], axis=1)  10.2 us
    all_to_all x2, starting transfers between devices, body(): lax.all_to_all(chosen, 'chan', split_axis=1, concat_axis=1, tiled=True)  9.53 us
  transfers between devices with their start and end apart: 5, of which 4 were waited for; matrix products, arithmetic and copies ran while one was open for 13% of the time, Pallas kernels for 0%

commit v1 on v0

--- a/solution.py
+++ b/solution.py
@@ -5,6 +5,34 @@
 
 HMAX = 12
 ROUNDS = 2
+
+
+def limits_unite(work_x, k_dim, chunk):
+    mid_arr, new = (work_x.shape[:k_dim], work_x.shape[k_dim + 1 :])
+    return jnp.moveaxis(work_x.reshape(*mid_arr, chunk, -1, *new), k_dim, 0)
+
+
+def unite_wall(z, d0):
+    z = jnp.moveaxis(z, 0, d0)
+    block_last = z.shape
+    return z.reshape(*block_last[:d0], block_last[d0] * block_last[d0 + 1], *block_last[d0 + 2 :])
+
+
+def attach_node(v0, local, target, mesh_ax):
+    x_new, near = (jax.lax.axis_size(mesh_ax), jax.lax.axis_index(mesh_ax))
+    newest = limits_unite(local, target, x_new)
+    m = 1
+    trail = [newest[near]]
+    while m < x_new:
+        next_value = newest[near ^ m]
+        trail.append(
+            jax.lax.ppermute(
+                next_value, axis_name=mesh_ax, perm=[(num, num ^ m) for num in range(x_new)]
+            )
+        )
+        m = m + 1
+    newest = jnp.stack(trail)[near ^ jnp.arange(x_new)]
+    return unite_wall(newest, v0)
 
 
 def padded_2(cells, sides, width):
@@ -57,7 +85,7 @@
     for step in range(ROUNDS):
         held = lax.all_to_all(sectioned, "chan", split_axis=1, concat_axis=1, tiled=True)
         chosen = jnp.take(held, partner[step], axis=1)
-        other = lax.all_to_all(chosen, "chan", split_axis=1, concat_axis=1, tiled=True)
+        other = attach_node(1, chosen, 1, "chan")
         results.append(pair_block(white, other.reshape(bins, chans, columns), windows))
     return jnp.stack(results)
 

time: 253 us -> 304 us (1.20)
  local copies, waits for them, and re-layouts: 25.3 us -> 62.2 us
  waiting for transfers between devices: 133 us -> 148 us
  other arithmetic: 47.6 us -> 44.5 us
    ppermute x0 -> x14, waiting for transfers between devices: none -> 95.3 us  [attach_node(): jax.lax.ppermute(next_value, axis_name=mesh_ax, perm=[(num, num ^ m) for...]
    all_to_all x2 -> x0, waiting for transfers between devices: 74.5 us -> none  [body(): lax.all_to_all(chosen, 'chan', split_axis=1, concat_axis=1, tiled=True)]
    unnamed x18 -> x40, local copies, waits for them, and re-layouts: 4.39 us -> 21.1 us
    ppermute x0 -> x14, starting transfers between devices: none -> 12.1 us  [attach_node(): jax.lax.ppermute(next_value, axis_name=mesh_ax, perm=[(num, num ^ m) for...]
    gather x0 -> x2, local copies, waits for them, and re-layouts: none -> 11.4 us  [attach_node(): newest = jnp.stack(trail)[near ^ jnp.arange(x_new)]]
    all_to_all x2 -> x0, starting transfers between devices: 9.53 us -> none  [body(): lax.all_to_all(chosen, 'chan', split_axis=1, concat_axis=1, tiled=True)]
    transpose x0 -> x2, local copies, waits for them, and re-layouts: none -> 8.67 us  [unite_wall(): z = jnp.moveaxis(z, 0, d0)]
    all_to_all x1, waiting for transfers between devices: 54.7 us -> 48.1 us  [body(): lax.all_to_all(sectioned, 'chan', split_axis=1, concat_axis=1, tiled=True)]
  transfers between devices with their start and end apart: 5 -> 17, of which waited for: 4 -> 6; matrix products, arithmetic and copies ran while one was open for 13% -> 15% of each run, Pallas kernels for 0% -> 0%
where the time goes in v1:
time: 304 us; the launch traced here: 303 us
  waiting for transfers between devices  148 us (49%)
  local copies, waits for them, and re-layouts  62.2 us (20%)
  other arithmetic  44.5 us (15%)
  matrix products  25.6 us (8%)
  starting transfers between devices  23.1 us (8%)
    ppermute x14, waiting for transfers between devices, attach_node(): jax.lax.ppermute(next_value, axis_name=mesh_ax, perm=[(num, num ^ m) for...  95.3 us
    all_to_all x1, waiting for transfers between devices, body(): lax.all_to_all(sectioned, 'chan', split_axis=1, concat_axis=1, tiled=True)  48.1 us
    dot_general x3, matrix products, pair_block(): jnp.einsum('fcw,fdw->fcd', own, right, preferred_element_type=jnp.float32)  25.6 us
    unnamed x40, local copies, waits for them, and re-layouts  21.1 us
    another operation x1, other arithmetic, body(): return jnp.stack(results)  16.5 us
    neg x3, other arithmetic, pair_block(): -other[:, :, windows:]  14.4 us
    ppermute x14, starting transfers between devices, attach_node(): jax.lax.ppermute(next_value, axis_name=mesh_ax, perm=[(num, num ^ m) for...  12.1 us
    gather x2, local copies, waits for them, and re-layouts, body(): chosen = jnp.take(held, partner[step], axis=1)  11.4 us
  transfers between devices with their start and end apart: 17, of which 6 were waited for; matrix products, arithmetic and copies ran while one was open for 15% of the time, Pallas kernels for 0%

profile of v1, /device:TPU:0, one launch (start us, length us, event | category | flops | bytes accessed | tf_op | source)
XLA Modules:
  0.0 303.2 jit_solution(1399749733346042968)
XLA Ops:
  0.0 3.4 %fusion = f32[24,256]{1,0:T(8,128)S(1)} fusion(bf16[24,256,384]{2,1,0:T(8,128)(2,1)} %param.5), kind=kLoop, calls=%fused_computation.10 | loop fusion | flops 7071744 | bytes 4743168 | tf_op jit(solution)/shard_map/reduce_sum | solution.py:66
  3.4 5.0 %collective-permute-start = (f32[12,256]{1,0:T(8,128)S(1)}, f32[12,256]{1,0:T(8,128)S(1)}, u32[]{:S(2)}, u32[]{:S(2)}) collective-permute-start(f32[12,256]{1,0:T(8,128)S(1)} %get-tuple-element.30), channel_id=1, source_target_pairs={{0,1},{1,2},{2,3},{4,5},{5,6},{6,7},{8,9},{9,10},{10,11},{12,13},{... | collective-permute-start | bytes 36872 | tf_op jit(solution)/shard_map/ppermute | solution.py:46
  8.3 1.3 collective-permute-start.1
  9.8 4.1 %collective-permute-done.1 = f32[12,256]{1,0:T(8,128)S(1)} collective-permute-done((f32[12,256]{1,0:T(8,128)S(1)}, f32[12,256]{1,0:T(8,128)S(1)}, u32[]{:S(2)}, u32[]{:S(2)}) %collective-permute-start.1) | collective-permute-done | bytes 12320 | tf_op jit(solution)/shard_map/ppermute | solution.py:48
  14.2 2.9 fusion.1
  17.1 2.2 copy-done
  19.3 2.7 copy.6
  22.0 4.7 %all-to-all-start = ((bf16[24,8,32,384]{3,2,0,1:T(8,128)(2,1)}), bf16[24,8,32,384]{3,2,0,1:T(8,128)(2,1)}, u32[]{:S(2)}, u32[]{:S(2)}) async-start(bf16[24,8,32,384]{3,2,0,1:T(8,128)(2,1)} %copy.6), calls=%async_computation | async-start | bytes 9437184 | tf_op jit(solution)/shard_map/all_to_all | solution.py:86
  26.9 6.5 %slice_negate_fusion.2 = (bf16[24,256,192]{2,1,0:T(8,128)(2,1)}, bf16[24,256,192]{2,1,0:T(8,128)(2,1)}) fusion(bf16[24,256,384]{2,1,0:T(8,128)(2,1)} %copy-done), kind=kLoop, calls=%fused_computation.37 | loop fusion | flops 1179648 | bytes 9437184 | tf_op jit(solution)/shard_map/neg | solution.py:56
  33.3 48.1 %all-to-all-done = bf16[24,8,32,384]{3,2,0,1:T(8,128)(2,1)} async-done(((bf16[24,8,32,384]{3,2,0,1:T(8,128)(2,1)}), bf16[24,8,32,384]{3,2,0,1:T(8,128)(2,1)}, u32[]{:S(2)}, u32[]{:S(2)}) %all-to-all-start) | async-done | bytes 4718624 | tf_op jit(solution)/shard_map/all_to_all | solution.py:86
  81.4 5.6 %gather_fusion.3 = bf16[8,24,32,384]{3,2,1,0:T(8,128)(2,1)} fusion(bf16[24,8,32,384]{3,2,0,1:T(8,128)(2,1)} %all-to-all-done, s32[1024]{0:T(1024)S(1)} %pad_clamp_fusion), kind=kCustom, calls=%fused_computation.1.clone | custom fusion | bytes 9437216 | tf_op jit(solution)/shard_map/jit(_take)/gather | solution.py:87
  87.1 5.8 %gather_fusion.2 = bf16[8,24,32,384]{3,2,1,0:T(8,128)(2,1)} fusion(bf16[24,8,32,384]{3,2,0,1:T(8,128)(2,1)} %all-to-all-done, s32[1024]{0:T(1024)S(1)} %pad_clamp_fusion.2), kind=kCustom, calls=%fused_computation.clone | custom fusion | bytes 9437216 | tf_op jit(solution)/shard_map/jit(_take)/gather | solution.py:87
  92.9 7.1 %select_bitcast_fusion = (bf16[24,8,32,384]{3,2,0,1:T(8,128)(2,1)S(1)}, bf16[24,8,32,384]{3,2,0,1:T(8,128)(2,1)}) fusion(bf16[8,24,32,384]{3,2,1,0:T(8,128)(2,1)} %gather_fusion.3, pred[8]{0:T(512)(128)(4,1)S(1)} %get-tuple-element.32, bf16[8,24,32,384]{3,2,1,0:T(8,128)(2,1)} %gather_fusion.2, pred[8]{0:T(512)(128)(4,1)S(1)} %get-tuple-element.6), kind=kLoop, calls=%fused_computation.33 | loop fusion | flops 4718592 | bytes 18874384 | tf_op jit(solution)/shard_map/jit(_take)/select_n | solution.py:87
  100.0 2.2 copy-done.2
  102.2 2.1 constant_dynamic-slice_fusion
  104.3 8.1 %fusion.20 = bf16[1,24,256,512]{3,2,1,0:T(8,128)(2,1)} fusion(bf16[24,256,384]{2,1,0:T(8,128)(2,1)S(1)} %bitcast.66, bf16[24,256,192]{2,1,0:T(8,128)(2,1)} %get-tuple-element.11, bf16[24,256,192]{2,1,0:T(8,128)(2,1)} %get-tuple-element.10), kind=kOutput, calls=%fused_computation.30 | convolution fusion | flops 2450522112 | bytes 15728640 | tf_op jit(solution)/shard_map/fcw,fdw->fcd/dot_general | solution.py:58
  113.0 2.3 collective-permute-start.14
  115.4 1.4 collective-permute-start.10
  116.7 1.9 bitcast_dynamic-update-slice_fusion.7
  118.7 2.9 constant_dynamic-slice_fusion.7
  121.6 1.9 bitcast_dynamic-update-slice_fusion.15
  124.0 2.0 bitcast_dynamic-update-slice_fusion.6
  126.0 40.1 %collective-permute-done.10 = bf16[24,1,32,384]{3,2,0,1:T(8,128)(2,1)S(1)} collective-permute-done((bf16[24,1,32,384]{3,2,0,1:T(8,128)(2,1)}, bf16[24,1,32,384]{3,2,0,1:T(8,128)(2,1)S(1)}, u32[]{:S(2)}, u32[]{:S(2)}) %collective-permute-start.10) | collective-permute-done | bytes 589856 | tf_op jit(solution)/shard_map/ppermute | solution.py:29
  166.7 0.9 bitcast_dynamic-update-slice_fusion.5
  167.6 1.3 collective-permute-start.8
  169.7 2.3 collective-permute-start.7
  173.0 34.0 %collective-permute-done.13 = bf16[24,1,32,384]{3,2,0,1:T(8,128)(2,1)S(1)} collective-permute-done((bf16[24,1,32,384]{3,2,0,1:T(8,128)(2,1)S(1)}, bf16[24,1,32,384]{3,2,0,1:T(8,128)(2,1)S(1)}, u32[]{:S(2)}, u32[]{:S(2)}) %collective-permute-start.13) | collective-permute-done | bytes 589856 | tf_op jit(solution)/shard_map/ppermute | solution.py:29
  207.1 0.9 bitcast_dynamic-update-slice_fusion.2
  209.5 1.1 collective-permute-start.4
  210.6 0.9 bitcast_dynamic-update-slice_fusion
  211.6 1.2 collective-permute-start.5
  212.7 0.9 bitcast_dynamic-update-slice_fusion.14
  213.6 10.6 %collective-permute-done.3 = bf16[24,1,32,384]{3,2,0,1:T(8,128)(2,1)S(1)} collective-permute-done((bf16[24,1,32,384]{3,2,0,1:T(8,128)(2,1)S(1)}, bf16[24,1,32,384]{3,2,0,1:T(8,128)(2,1)S(1)}, u32[]{:S(2)}, u32[]{:S(2)}) %collective-permute-start.3) | collective-permute-done | bytes 589856 | tf_op jit(solution)/shard_map/ppermute | solution.py:29
  224.2 0.9 bitcast_dynamic-update-slice_fusion.13
  225.1 10.6 %collective-permute-done.4 = bf16[24,1,32,384]{3,2,0,1:T(8,128)(2,1)S(1)} collective-permute-done((bf16[24,1,32,384]{3,2,0,1:T(8,128)(2,1)S(1)}, bf16[24,1,32,384]{3,2,0,1:T(8,128)(2,1)S(1)}, u32[]{:S(2)}, u32[]{:S(2)}) %collective-permute-start.4) | collective-permute-done | bytes 589856 | tf_op jit(solution)/shard_map/ppermute | solution.py:29
  235.7 1.0 bitcast_dynamic-update-slice_fusion.12
  237.5 5.7 %gather_fusion.1 = bf16[8,24,32,384]{3,2,1,0:T(8,128)(2,1)} fusion(bf16[8,24,32,384]{3,2,1,0:T(8,128)(2,1)} %bitcast.28, s32[1024]{0:T(1024)S(1)} %pad_clamp_fusion.1), kind=kCustom, calls=%fused_computation.3 | custom fusion | bytes 9437216 | tf_op jit(solution)/shard_map/gather | solution.py:34
  243.2 5.3 %copy.8 = bf16[24,8,1,32,384]{4,3,1,0,2:T(8,128)(2,1)} copy(bf16[24,8,1,32,384]{4,3,0,1,2:T(8,128)(2,1)} %bitcast.76) | data formatting | bytes 9437184 | tf_op jit(solution)/shard_map/transpose | solution.py:16
  249.4 0.9 bitcast_dynamic-update-slice_fusion.9
  250.3 0.9 bitcast_dynamic-update-slice_fusion.8
  251.2 5.7 %gather_fusion = bf16[8,24,32,384]{3,2,1,0:T(8,128)(2,1)} fusion(bf16[8,24,32,384]{3,2,1,0:T(8,128)(2,1)} %bitcast.12, s32[1024]{0:T(1024)S(1)} %pad_clamp_fusion.1), kind=kCustom, calls=%fused_computation.2 | custom fusion | bytes 9437216 | tf_op jit(solution)/shard_map/gather | solution.py:34
  256.9 3.3 %copy.7 = bf16[24,8,1,32,384]{4,3,1,0,2:T(8,128)(2,1)S(1)} copy(bf16[24,8,1,32,384]{4,3,0,1,2:T(8,128)(2,1)} %bitcast.75) | data formatting | bytes 9437184 | tf_op jit(solution)/shard_map/transpose | solution.py:16
  260.3 4.1 %slice_negate_fusion.1 = (bf16[24,256,192]{2,1,0:T(8,128)(2,1)}, bf16[24,256,192]{2,1,0:T(8,128)(2,1)}) fusion(bf16[24,256,384]{2,1,0:T(8,128)(2,1)S(1)} %bitcast.73), kind=kLoop, calls=%fused_computation.36 | loop fusion | flops 1179648 | bytes 9437184 | tf_op jit(solution)/shard_map/neg | solution.py:56
  264.4 1.0 copy-done.1
  265.3 3.8 %slice_negate_fusion = (bf16[24,256,192]{2,1,0:T(8,128)(2,1)}, bf16[24,256,192]{2,1,0:T(8,128)(2,1)}) fusion(bf16[24,256,384]{2,1,0:T(8,128)(2,1)S(1)} %bitcast.72), kind=kLoop, calls=%fused_computation.35 | loop fusion | flops 1179648 | bytes 9437184 | tf_op jit(solution)/shard_map/neg | solution.py:56
  269.2 8.8 %fusion.21 = bf16[1,24,256,512]{3,2,1,0:T(8,128)(2,1)} fusion(bf16[24,256,384]{2,1,0:T(8,128)(2,1)S(1)} %bitcast.68, bf16[24,256,192]{2,1,0:T(8,128)(2,1)} %get-tuple-element.13, bf16[24,256,192]{2,1,0:T(8,128)(2,1)} %get-tuple-element.12, bf16[24,256,384]{2,1,0:T(8,128)(2,1)} %bitcast.74), kind=kOutput, calls=%fused_computation.31 | convolution fusion | flops 2450522112 | bytes 20447232 | tf_op jit(solution)/shard_map/fcw,fdw->fcd/dot_general | solution.py:58
  278.0 8.8 %fusion.22 = bf16[1,24,256,512]{3,2,1,0:T(8,128)(2,1)} fusion(bf16[24,256,384]{2,1,0:T(8,128)(2,1)S(1)} %bitcast.68, bf16[24,256,192]{2,1,0:T(8,128)(2,1)} %get-tuple-element.22, bf16[24,256,192]{2,1,0:T(8,128)(2,1)} %get-tuple-element.21, bf16[24,256,384]{2,1,0:T(8,128)(2,1)} %bitcast.69), kind=kOutput, calls=%fused_computation.32 | convolution fusion | flops 2450522112 | bytes 20447232 | tf_op jit(solution)/shard_map/fcw,fdw->fcd/dot_general | solution.py:58
  286.7 16.5 %pad_maximum_fusion = bf16[3,24,256,512]{3,2,1,0:T(8,128)(2,1)} fusion(bf16[1,24,256,512]{3,2,1,0:T(8,128)(2,1)} %fusion.22, bf16[1,24,256,512]{3,2,1,0:T(8,128)(2,1)} %fusion.21, bf16[1,24,256,512]{3,2,1,0:T(8,128)(2,1)} %fusion.20), kind=kLoop, calls=%fused_computation.4 | loop fusion | flops 18874368 | bytes 37748736 | tf_op jit(solution)/shard_map/stack | solution.py:90
  (61 shorter events, 7.3 us)
Async XLA Ops:
  0.0 9.7 %copy-start.5 = (s32[256]{0:T(256)S(1)}, s32[256]{0:T(256)}, u32[]{:S(2)}) copy-start(s32[256]{0:T(256)} %param.6) | copy-start | bytes 3076
  3.4 6.5 %collective-permute-start = (f32[12,256]{1,0:T(8,128)S(1)}, f32[12,256]{1,0:T(8,128)S(1)}, u32[]{:S(2)}, u32[]{:S(2)}) collective-permute-start(f32[12,256]{1,0:T(8,128)S(1)} %get-tuple-element.30), channel_id=1, source_target_pairs={{0,1},{1,2},{2,3},{4,5},{5,6},{6,7},{8,9},{9,10},{10,11},{12,13},{... | collective-permute-start | bytes 36872 | tf_op jit(solution)/shard_map/ppermute | solution.py:46
  8.3 5.6 %collective-permute-start.1 = (f32[12,256]{1,0:T(8,128)S(1)}, f32[12,256]{1,0:T(8,128)S(1)}, u32[]{:S(2)}, u32[]{:S(2)}) collective-permute-start(f32[12,256]{1,0:T(8,128)S(1)} %get-tuple-element.31), channel_id=1, source_target_pairs={{1,0},{2,1},{3,2},{5,4},{6,5},{7,6},{9,8},{10,9},{11,10},{13,12},{... | collective-permute-start | bytes 36872 | tf_op jit(solution)/shard_map/ppermute | solution.py:48
  17.1 2.2 copy-start
  22.0 4.8 %copy-start.6 = (s32[2,8]{1,0:T(2,128)S(1)}, s32[2,8]{1,0:T(2,128)}, u32[]{:S(2)}) copy-start(s32[2,8]{1,0:T(2,128)} %param.7) | copy-start | bytes 196
  22.0 59.5 %all-to-all-start = ((bf16[24,8,32,384]{3,2,0,1:T(8,128)(2,1)}), bf16[24,8,32,384]{3,2,0,1:T(8,128)(2,1)}, u32[]{:S(2)}, u32[]{:S(2)}) async-start(bf16[24,8,32,384]{3,2,0,1:T(8,128)(2,1)} %copy.6), calls=%async_computation | async-start | bytes 9437184 | tf_op jit(solution)/shard_map/all_to_all | solution.py:86
  87.1 17.2 %slice-start = ((s8[4718592]{0:T(1024)(128)(4,1)}), s8[524288]{0:T(1024)(128)(4,1)S(1)}, s32[]{:S(2)}) async-start(s8[4718592]{0:T(1024)(128)(4,1)} %bitcast.65), calls=%async_computation.1 | async-start | bytes 1048576
  92.9 11.4 %slice-start.1 = ((s8[4718592]{0:T(1024)(128)(4,1)}), s8[4194304]{0:T(1024)(128)(4,1)S(1)}, s32[]{:S(2)}) async-start(s8[4718592]{0:T(1024)(128)(4,1)} %bitcast.65), calls=%async_computation.2 | async-start | bytes 8388608
  100.0 2.2 copy-start.2
  104.3 19.2 %collective-permute-start.9 = (bf16[24,1,32,384]{3,2,0,1:T(8,128)(2,1)}, bf16[24,1,32,384]{3,2,0,1:T(8,128)(2,1)}, u32[]{:S(2)}, u32[]{:S(2)}) collective-permute-start(bf16[24,1,32,384]{3,2,0,1:T(8,128)(2,1)} %get-tuple-element.29), channel_id=1, source_target_pairs={{0,4},{4,0},{8,12},{12,8},{16,20},{20,16},{24,28},{28,24},{1,5},{5... | collective-permute-start | bytes 1769480 | tf_op jit(solution)/shard_map/ppermute | solution.py:29
  112.3 97.1 %collective-permute-start.15 = (bf16[24,1,32,384]{3,2,0,1:T(8,128)(2,1)}, bf16[24,1,32,384]{3,2,0,1:T(8,128)(2,1)S(1)}, u32[]{:S(2)}, u32[]{:S(2)}) collective-permute-start(bf16[24,1,32,384]{3,2,0,1:T(8,128)(2,1)} %get-tuple-element.23), channel_id=1, source_target_pairs={{0,28},{4,24},{8,20},{12,16},{16,12},{20,8},{24,4},{28,0},{1,29},{... | collective-permute-start | bytes 1769480 | tf_op jit(solution)/shard_map/ppermute | solution.py:29
  113.0 95.0 %collective-permute-start.14 = (bf16[24,1,32,384]{3,2,0,1:T(8,128)(2,1)}, bf16[24,1,32,384]{3,2,0,1:T(8,128)(2,1)S(1)}, u32[]{:S(2)}, u32[]{:S(2)}) collective-permute-start(bf16[24,1,32,384]{3,2,0,1:T(8,128)(2,1)} %get-tuple-element.24), channel_id=1, source_target_pairs={{0,24},{4,28},{8,16},{12,20},{16,8},{20,12},{24,0},{28,4},{1,25},{... | collective-permute-start | bytes 1769480 | tf_op jit(solution)/shard_map/ppermute | solution.py:29
  115.4 52.2 %collective-permute-start.11 = (bf16[24,1,32,384]{3,2,0,1:T(8,128)(2,1)}, bf16[24,1,32,384]{3,2,0,1:T(8,128)(2,1)S(1)}, u32[]{:S(2)}, u32[]{:S(2)}) collective-permute-start(bf16[24,1,32,384]{3,2,0,1:T(8,128)(2,1)} %get-tuple-element.27), channel_id=1, source_target_pairs={{0,12},{4,8},{8,4},{12,0},{16,28},{20,24},{24,20},{28,16},{1,13},{... | collective-permute-start | bytes 1769480 | tf_op jit(solution)/shard_map/ppermute | solution.py:29
  115.4 50.8 %collective-permute-start.10 = (bf16[24,1,32,384]{3,2,0,1:T(8,128)(2,1)}, bf16[24,1,32,384]{3,2,0,1:T(8,128)(2,1)S(1)}, u32[]{:S(2)}, u32[]{:S(2)}) collective-permute-start(bf16[24,1,32,384]{3,2,0,1:T(8,128)(2,1)} %get-tuple-element.28), channel_id=1, source_target_pairs={{0,8},{4,12},{8,0},{12,4},{16,24},{20,28},{24,16},{28,20},{1,9},{5... | collective-permute-start | bytes 1769480 | tf_op jit(solution)/shard_map/ppermute | solution.py:29
  118.7 4.8 %copy-start.4 = (bf16[24,1,32,384]{3,2,0,1:T(8,128)(2,1)S(1)}, bf16[24,1,32,384]{3,2,0,1:T(8,128)(2,1)}, u32[]{:S(2)}) copy-start(bf16[24,1,32,384]{3,2,0,1:T(8,128)(2,1)} %get-tuple-element.26) | copy-start | bytes 1769476
  118.7 47.4 %copy-start.3 = (bf16[24,1,32,384]{3,2,0,1:T(8,128)(2,1)S(1)}, bf16[24,1,32,384]{3,2,0,1:T(8,128)(2,1)}, u32[]{:S(2)}) copy-start(bf16[24,1,32,384]{3,2,0,1:T(8,128)(2,1)} %get-tuple-element.25) | copy-start | bytes 1769476
  123.5 46.2 %collective-permute-start.12 = (bf16[24,1,32,384]{3,2,0,1:T(8,128)(2,1)S(1)}, bf16[24,1,32,384]{3,2,0,1:T(8,128)(2,1)S(1)}, u32[]{:S(2)}, u32[]{:S(2)}) collective-permute-start(bf16[24,1,32,384]{3,2,0,1:T(8,128)(2,1)S(1)} %copy-done.4), channel_id=1, source_target_pairs={{0,16},{4,20},{8,24},{12,28},{16,0},{20,4},{24,8},{28,12},{1,17},{... | collective-permute-start | bytes 1769480 | tf_op jit(solution)/shard_map/ppermute | solution.py:29
  166.1 40.9 %collective-permute-start.13 = (bf16[24,1,32,384]{3,2,0,1:T(8,128)(2,1)S(1)}, bf16[24,1,32,384]{3,2,0,1:T(8,128)(2,1)S(1)}, u32[]{:S(2)}, u32[]{:S(2)}) collective-permute-start(bf16[24,1,32,384]{3,2,0,1:T(8,128)(2,1)S(1)} %copy-done.3), channel_id=1, source_target_pairs={{0,20},{4,16},{8,28},{12,24},{16,4},{20,0},{24,12},{28,8},{1,21},{... | collective-permute-start | bytes 1769480 | tf_op jit(solution)/shard_map/ppermute | solution.py:29
  167.6 82.7 %collective-permute-start.8 = (bf16[24,1,32,384]{3,2,0,1:T(8,128)(2,1)S(1)}, bf16[24,1,32,384]{3,2,0,1:T(8,128)(2,1)S(1)}, u32[]{:S(2)}, u32[]{:S(2)}) collective-permute-start(bf16[24,1,32,384]{3,2,0,1:T(8,128)(2,1)S(1)} %get-tuple-element.14), channel_id=1, source_target_pairs={{0,28},{4,24},{8,20},{12,16},{16,12},{20,8},{24,4},{28,0},{1,29},{... | collective-permute-start | bytes 1769480 | tf_op jit(solution)/shard_map/ppermute | solution.py:29
  169.7 79.7 %collective-permute-start.7 = (bf16[24,1,32,384]{3,2,0,1:T(8,128)(2,1)S(1)}, bf16[24,1,32,384]{3,2,0,1:T(8,128)(2,1)S(1)}, u32[]{:S(2)}, u32[]{:S(2)}) collective-permute-start(bf16[24,1,32,384]{3,2,0,1:T(8,128)(2,1)S(1)} %get-tuple-element.15), channel_id=1, source_target_pairs={{0,24},{4,28},{8,16},{12,20},{16,8},{20,12},{24,0},{28,4},{1,25},{... | collective-permute-start | bytes 1769480 | tf_op jit(solution)/shard_map/ppermute | solution.py:29
  207.0 4.6 %collective-permute-start.2 = (bf16[24,1,32,384]{3,2,0,1:T(8,128)(2,1)S(1)}, bf16[24,1,32,384]{3,2,0,1:T(8,128)(2,1)S(1)}, u32[]{:S(2)}, u32[]{:S(2)}) collective-permute-start(bf16[24,1,32,384]{3,2,0,1:T(8,128)(2,1)S(1)} %get-tuple-element.20), channel_id=1, source_target_pairs={{0,4},{4,0},{8,12},{12,8},{16,20},{20,16},{24,28},{28,24},{1,5},{5... | collective-permute-start | bytes 1769480 | tf_op jit(solution)/shard_map/ppermute | solution.py:29
  208.0 16.2 %collective-permute-start.3 = (bf16[24,1,32,384]{3,2,0,1:T(8,128)(2,1)S(1)}, bf16[24,1,32,384]{3,2,0,1:T(8,128)(2,1)S(1)}, u32[]{:S(2)}, u32[]{:S(2)}) collective-permute-start(bf16[24,1,32,384]{3,2,0,1:T(8,128)(2,1)S(1)} %get-tuple-element.19), channel_id=1, source_target_pairs={{0,8},{4,12},{8,0},{12,4},{16,24},{20,28},{24,16},{28,20},{1,9},{5... | collective-permute-start | bytes 1769480 | tf_op jit(solution)/shard_map/ppermute | solution.py:29
  209.5 26.2 %collective-permute-start.4 = (bf16[24,1,32,384]{3,2,0,1:T(8,128)(2,1)S(1)}, bf16[24,1,32,384]{3,2,0,1:T(8,128)(2,1)S(1)}, u32[]{:S(2)}, u32[]{:S(2)}) collective-permute-start(bf16[24,1,32,384]{3,2,0,1:T(8,128)(2,1)S(1)} %get-tuple-element.18), channel_id=1, source_target_pairs={{0,12},{4,8},{8,4},{12,0},{16,28},{20,24},{24,20},{28,16},{1,13},{... | collective-permute-start | bytes 1769480 | tf_op jit(solution)/shard_map/ppermute | solution.py:29
  211.6 25.1 %collective-permute-start.5 = (bf16[24,1,32,384]{3,2,0,1:T(8,128)(2,1)S(1)}, bf16[24,1,32,384]{3,2,0,1:T(8,128)(2,1)S(1)}, u32[]{:S(2)}, u32[]{:S(2)}) collective-permute-start(bf16[24,1,32,384]{3,2,0,1:T(8,128)(2,1)S(1)} %get-tuple-element.17), channel_id=1, source_target_pairs={{0,16},{4,20},{8,24},{12,28},{16,0},{20,4},{24,8},{28,12},{1,17},{... | collective-permute-start | bytes 1769480 | tf_op jit(solution)/shard_map/ppermute | solution.py:29
  224.2 24.4 %collective-permute-start.6 = (bf16[24,1,32,384]{3,2,0,1:T(8,128)(2,1)S(1)}, bf16[24,1,32,384]{3,2,0,1:T(8,128)(2,1)S(1)}, u32[]{:S(2)}, u32[]{:S(2)}) collective-permute-start(bf16[24,1,32,384]{3,2,0,1:T(8,128)(2,1)S(1)} %get-tuple-element.16), channel_id=1, source_target_pairs={{0,20},{4,16},{8,28},{12,24},{16,4},{20,0},{24,12},{28,8},{1,21},{... | collective-permute-start | bytes 1769480 | tf_op jit(solution)/shard_map/ppermute | solution.py:29
  256.9 8.5 %slice-start.4 = ((s8[4718592]{0:T(1024)(128)(4,1)}), s8[4194304]{0:T(1024)(128)(4,1)S(1)}, s32[]{:S(2)}) async-start(s8[4718592]{0:T(1024)(128)(4,1)} %bitcast.70), calls=%async_computation.5 | async-start | bytes 8388608
  260.2 5.1 %copy-start.1 = (bf16[24,8,1,32,384]{4,3,1,0,2:T(8,128)(2,1)}, bf16[24,8,1,32,384]{4,3,1,0,2:T(8,128)(2,1)S(1)}, u32[]{:S(2)}) copy-start(bf16[24,8,1,32,384]{4,3,1,0,2:T(8,128)(2,1)S(1)} %copy.7) | copy-start | bytes 14155780
  260.2 5.1 %slice-start.5 = ((s8[4718592]{0:T(1024)(128)(4,1)}), s8[524288]{0:T(1024)(128)(4,1)S(1)}, s32[]{:S(2)}) async-start(s8[4718592]{0:T(1024)(128)(4,1)} %bitcast.70), calls=%async_computation.6 | async-start | bytes 1048576
  260.2 8.9 %slice-start.2 = ((s8[4718592]{0:T(1024)(128)(4,1)}), s8[4194304]{0:T(1024)(128)(4,1)S(1)}, s32[]{:S(2)}) async-start(s8[4718592]{0:T(1024)(128)(4,1)} %bitcast.67), calls=%async_computation.3 | async-start | bytes 8388608
  265.3 3.8 %slice-start.3 = ((s8[4718592]{0:T(1024)(128)(4,1)}), s8[524288]{0:T(1024)(128)(4,1)S(1)}, s32[]{:S(2)}) async-start(s8[4718592]{0:T(1024)(128)(4,1)} %bitcast.67), calls=%async_computation.4 | async-start | bytes 1048576
